TPU v7x, 128 devices: a whole 4x4x4 slice. The times are simulated.
128 devices in a mesh: batch: 8 (over x, core), item: 16 (over z, y).
Axes of the slice: x: 4, y: 4, z: 4, core: 2. Of those that a mesh axis runs over, the one named last changes fastest.
Arguments:
- user_vectors: bfloat16 [32768, 512], P(('batch', 'item')), may hold values from -6 to 6
- item_table: bfloat16 [524288, 512], P(('batch', 'item')), may hold values from -0.25 to 0.25
- tower_weight: bfloat16 [512, 512], replicated, may hold values from -3 to 3
- item_owner: int32 [32768, 1], P(('batch', 'item')), may hold values from 0 to 127; in each aligned block of 256 rows (0 to 255, 256 to 511, ...) at most 4 rows name the same one
- item_row: int32 [32768], P(('batch', 'item')), may hold values from 0 to 4095
Outputs:
- table_grad: bfloat16 [524288, 512], P(('batch', 'item'))
- weight_grad: float32 [512, 512], P(('batch', 'item'))
Inputs may be any that keep to these rules, and one draw needn't show every extreme that they name: `item_owner`: within the rows of one device (aligned blocks of 256 rows) no owner is named by more than 4 rows, a bound that some block reaches.
All inputs are finite; a program needn't handle non-finite values.
Results may differ from a plain program's by a relative error of at most 0.0075.
Values may be sent and summed in bfloat16 or wider, within the bound.
A program may use at most 64 MiB of HBM per device.

v0:
```python
import jax
import jax.numpy as jnp
from jax import lax
from jax.sharding import PartitionSpec as P

epsilon = 1e-06
score_scale = 60.0
cauchy_scale = 4.0


def local(user_vectors, item_table, tower_weight, item_owner, item_row):
    b_dev, width = user_vectors.shape
    n_batch = lax.axis_size("batch")
    n_item = lax.axis_size("item")
    devices = n_batch * n_item
    slots = 2 * b_dev // devices
    owner = item_owner[:, 0]
    onehot = (owner[:, None] == jnp.arange(devices, dtype=jnp.int32)[None, :]).astype(jnp.int32)
    rank = jnp.sum(jnp.cumsum(onehot, axis=0) * onehot, axis=1) - 1
    place = owner * slots + rank
    request = (
        jnp.zeros((devices * slots,), jnp.int32).at[place].set(item_row).reshape(devices, slots)
    )
    asked = lax.all_to_all(request, ("batch", "item"), split_axis=0, concat_axis=0, tiled=True)
    found = item_table[asked]
    back = lax.all_to_all(found, ("batch", "item"), split_axis=0, concat_axis=0, tiled=True)
    fetched, asked = (back, asked)
    embed = fetched.reshape(devices * slots, width)[place]
    hidden = jnp.dot(embed, tower_weight, preferred_element_type=jnp.float32)
    rscale = lax.rsqrt(jnp.mean(hidden * hidden, axis=1, keepdims=True) + epsilon)
    item_vec = (hidden * rscale / jnp.sqrt(jnp.float32(width))).astype(jnp.bfloat16)
    user_f = user_vectors.astype(jnp.float32)
    user_unit = (
        user_f
        * lax.rsqrt(jnp.mean(user_f * user_f, axis=1, keepdims=True) + epsilon)
        / jnp.sqrt(jnp.float32(width))
    ).astype(jnp.bfloat16)
    piece = lax.all_gather(user_unit, "batch", axis=0, tiled=True)
    score = (
        lax.dot_general(
            item_vec, piece, (((1,), (1,)), ((), ())), preferred_element_type=jnp.float32
        )
        * score_scale
    )
    expo = jnp.exp(score)
    partial_mix = jnp.dot(expo.astype(jnp.bfloat16), piece, preferred_element_type=jnp.float32)
    total = jnp.sum(expo, axis=1)
    unit_f = user_unit.astype(jnp.float32)
    positive = jnp.sum(item_vec.astype(jnp.float32) * unit_f, axis=1) * score_scale
    xent = jnp.log(total) - positive
    cweight = 1.0 / (1.0 + xent / cauchy_scale)
    dvec = cweight[:, None] * score_scale * (partial_mix / total[:, None] - unit_f)
    inner = jnp.sum(hidden * dvec, axis=1, keepdims=True)
    dhidden = (
        rscale / jnp.sqrt(jnp.float32(width)) * (dvec - hidden * rscale * rscale * inner / width)
    ).astype(jnp.bfloat16)
    weight_grad = lax.psum_scatter(
        lax.dot_general(
            embed, dhidden, (((0,), (0,)), ((), ())), preferred_element_type=jnp.float32
        ),
        ("batch", "item"),
        scatter_dimension=0,
        tiled=True,
    )
    drow = jnp.dot(dhidden, tower_weight.T, preferred_element_type=jnp.float32)
    outgoing = jnp.zeros((devices * slots, width), jnp.float32).at[place].set(drow)
    incoming = lax.all_to_all(
        outgoing.reshape(devices, slots, width).astype(jnp.bfloat16),
        ("batch", "item"),
        split_axis=0,
        concat_axis=0,
        tiled=True,
    ).astype(jnp.float32)
    arrived = incoming.reshape(devices * slots, width)
    table_grad = (
        jnp.zeros((item_table.shape[0], width), jnp.float32).at[asked.reshape(-1)].add(arrived)
    )
    return (table_grad.astype(jnp.bfloat16), weight_grad)


def solution(mesh):
    return jax.shard_map(
        local,
        mesh=mesh,
        in_specs=(
            P(("batch", "item"), None),
            P(("batch", "item"), None),
            P(),
            P(("batch", "item"), None),
            P(("batch", "item")),
        ),
        out_specs=(P(("batch", "item"), None), P(("batch", "item"), None)),
        check_vma=False,
    )
```

profile of v0, /device:TPU:0, one launch (start us, length us, event | category | flops | bytes accessed | tf_op | source)
XLA Modules:
  0.0 243.8 jit_solution(17994513546542418527)
XLA Ops:
  7.2 0.8 copy.10
  8.0 0.2 fusion.12
  8.3 0.9 fusion.13
  9.2 0.7 compare_select_fusion.2
  9.9 1.6 scatter_custom_fusion
  11.6 20.5 %all_to_all.22 = s32[128,1,4]{2,1,0:T(1,128)S(1)} all-to-all(s32[128,1,4]{2,1,0:T(1,128)S(1)} %bitcast.34), channel_id=1, replica_groups=mesh['batch'=8,'item'=16] {'batch','item'}, dimensions={0} | all-to-all | bytes 4096 | tf_op jit(solution)/shard_map/all_to_all | solution.py:24
  32.2 4.7 %gather_fusion = bf16[512,512]{1,0:T(8,128)(2,1)S(1)} fusion(bf16[4096,512]{1,0:T(8,128)(2,1)} %param.6, s32[1024]{0:T(1024)S(1)} %pad_clamp_fusion.1), kind=kCustom, calls=%fused_computation | custom fusion | bytes 1050624 | tf_op jit(solution)/shard_map/gather | solution.py:25
  36.9 0.9 reshape.146
  37.8 4.6 %all-to-all-start.1 = ((bf16[128,4,512]{2,1,0:T(4,128)(2,1)}), bf16[128,4,512]{2,1,0:T(4,128)(2,1)S(1)}, u32[]{:S(2)}, u32[]{:S(2)}) async-start(bf16[128,4,512]{2,1,0:T(4,128)(2,1)} %reshape.146), calls=%async_computation.1 | async-start | bytes 1048576 | tf_op jit(solution)/shard_map/all_to_all | solution.py:26
  42.5 0.1 fusion.6
  42.7 13.4 %all-to-all-done.1 = bf16[128,4,512]{2,1,0:T(4,128)(2,1)S(1)} async-done(((bf16[128,4,512]{2,1,0:T(4,128)(2,1)}), bf16[128,4,512]{2,1,0:T(4,128)(2,1)S(1)}, u32[]{:S(2)}, u32[]{:S(2)}) %all-to-all-start.1) | async-done | bytes 524320 | tf_op jit(solution)/shard_map/all_to_all | solution.py:26
  56.0 0.1 reshape.140
  56.2 1.2 gather_fusion.1
  57.3 0.4 multiply_reduce_fusion.1
  57.7 0.9 fusion.9
  58.7 21.1 %all-gather.2.cloned.1.call-done = bf16[2048,512]{1,0:T(8,128)(2,1)} async-done(((bf16[256,512]{1,0:T(8,128)(2,1)}), bf16[2048,512]{1,0:T(8,128)(2,1)}) %all-gather.2.cloned.1.call-update) | async-done | bytes 2097168 | tf_op jit(solution)/shard_map/all_gather | solution.py:38
  79.8 2.6 %fusion.19 = (f32[256]{0:T(256)S(1)}, bf16[256,2048]{1,0:T(8,128)(2,1)S(1)}) fusion(bf16[2048,512]{1,0:T(8,128)(2,1)} %all-gather.2.cloned.1.call-done, f32[256,512]{1,0:T(8,128)S(1)} %get-tuple-element.7, f32[256]{0:T(256)S(1)} %get-tuple-element.5), kind=kOutput, calls=%fused_computation.48 | convolution fusion | flops 538836736 | bytes 3672064 | tf_op jit(solution)/shard_map/dot_general | solution.py:40
  82.5 0.8 multiply_reduce_fusion
  83.3 0.2 multiply_convert_fusion
  83.5 1.3 fusion.21
  84.8 0.3 fusion.20
  85.2 1.7 scatter_custom_fusion.1
  86.9 0.9 convert_element_type.45
  87.8 9.3 %all-to-all-start.2 = ((bf16[128,4,512]{2,1,0:T(4,128)(2,1)}), bf16[128,4,512]{2,1,0:T(4,128)(2,1)S(1)}, u32[]{:S(2)}, u32[]{:S(2)}) async-start(bf16[128,4,512]{2,1,0:T(4,128)(2,1)} %convert_element_type.45), calls=%async_computation.2 | async-start | bytes 1048576 | tf_op jit(solution)/shard_map/all_to_all | solution.py:67
  97.1 0.5 broadcast.185
  97.6 0.8 reduce.3
  98.5 0.1 reshape.139
  98.6 12.5 %all-to-all-done.2 = bf16[128,4,512]{2,1,0:T(4,128)(2,1)S(1)} async-done(((bf16[128,4,512]{2,1,0:T(4,128)(2,1)}), bf16[128,4,512]{2,1,0:T(4,128)(2,1)S(1)}, u32[]{:S(2)}, u32[]{:S(2)}) %all-to-all-start.2) | async-done | bytes 524320 | tf_op jit(solution)/shard_map/all_to_all | solution.py:67
  111.1 7.3 %scatter_custom_fusion.2 = f32[4096,512]{1,0:T(8,128)} fusion(s32[512]{0:T(512)S(1)} %bitcast.42, f32[512,512]{1,0:T(8,128)S(1)} %reshape.181, f32[]{:T(128)} %constant.12.clone.1), kind=kCustom, calls=%fused_computation.5 | custom fusion | flops 262144 | bytes 8388612 | tf_op jit(solution)/shard_map/scatter-add | solution.py:76
  118.4 6.0 %convert_element_type.46 = bf16[4096,512]{1,0:T(8,128)(2,1)} convert(f32[4096,512]{1,0:T(8,128)} %scatter_custom_fusion.2) | non-fusion elementwise | flops 2097152 | bytes 12582912 | tf_op jit(solution)/shard_map/convert_element_type | solution.py:78
  124.4 111.3 %all-reduce.3.cloned.1.call-done = f32[512,512]{1,0:T(8,128)} async-done(((f32[512,512]{1,0:T(8,128)}), f32[512,512]{1,0:T(8,128)}) %all-reduce.3.cloned.1.call-update) | async-done | bytes 1048592
  235.7 1.3 constant_dynamic-slice_fusion
  (29 shorter events, 0.6 us)
Async XLA Ops:
  7.2 50.2 %copy-start = (bf16[512,512]{1,0:T(8,128)(2,1)S(1)}, bf16[512,512]{1,0:T(8,128)(2,1)}, u32[]{:S(2)}) copy-start(bf16[512,512]{1,0:T(8,128)(2,1)} %param.7) | copy-start | bytes 1572868
  36.9 5.6 %copy-start.1 = (bf16[256,512]{1,0:T(8,128)(2,1)S(1)}, bf16[256,512]{1,0:T(8,128)(2,1)}, u32[]{:S(2)}) copy-start(bf16[256,512]{1,0:T(8,128)(2,1)} %param.5) | copy-start | bytes 786436
  37.8 18.2 %all-to-all-start.1 = ((bf16[128,4,512]{2,1,0:T(4,128)(2,1)}), bf16[128,4,512]{2,1,0:T(4,128)(2,1)S(1)}, u32[]{:S(2)}, u32[]{:S(2)}) async-start(bf16[128,4,512]{2,1,0:T(4,128)(2,1)} %reshape.146), calls=%async_computation.1 | async-start | bytes 1048576 | tf_op jit(solution)/shard_map/all_to_all | solution.py:26
  42.5 37.4 %all-gather.2.cloned.1.call-start = ((), (), s32[]{:S(2)}) async-start(), calls=%async_computation.3 | async-start | bytes 2359296 | tf_op jit(solution)/shard_map/all_gather | solution.py:38
  58.7 23.8 %copy-start.2 = (bf16[256,512]{1,0:T(8,128)(2,1)S(1)}, bf16[256,512]{1,0:T(8,128)(2,1)}, u32[]{:S(2)}) copy-start(bf16[256,512]{1,0:T(8,128)(2,1)} %get-tuple-element.3) | copy-start | bytes 786436
  58.7 177.0 %all-reduce.3.cloned.1.call-start = ((), (), s32[]{:S(2)}) async-start(), calls=%async_computation.4 | async-start | bytes 2097152
  79.8 2.6 %copy-start.3 = (bf16[2048,512]{1,0:T(8,128)(2,1)S(1)}, bf16[2048,512]{1,0:T(8,128)(2,1)}, u32[]{:S(2)}) copy-start(bf16[2048,512]{1,0:T(8,128)(2,1)} %all-gather.2.cloned.1.call-done) | copy-start | bytes 6291460
  87.8 23.2 %all-to-all-start.2 = ((bf16[128,4,512]{2,1,0:T(4,128)(2,1)}), bf16[128,4,512]{2,1,0:T(4,128)(2,1)S(1)}, u32[]{:S(2)}, u32[]{:S(2)}) async-start(bf16[128,4,512]{2,1,0:T(4,128)(2,1)} %convert_element_type.45), calls=%async_computation.2 | async-start | bytes 1048576 | tf_op jit(solution)/shard_map/all_to_all | solution.py:67
Sparse Core Ops, SparseCore 0:
  58.8 21.0 all-gather.1
  85.0 150.6 all-reduce.2
where the time goes:
time: 246 us; the launch traced here: 244 us
  waiting for transfers between devices  158 us (64%)
  blocking collectives  20.5 us (8%)
  other arithmetic  17.2 us (7%)
  between operations  14.3 us (6%)
  local copies, waits for them, and re-layouts  14.2 us (6%)
  starting transfers between devices  14 us (6%)
  matrix products  5.44 us (2%)
    unnamed x3, waiting for transfers between devices  111 us
    all_gather x1, waiting for transfers between devices, local(): piece = lax.all_gather(user_unit, 'batch', axis=0, tiled=True)  21.1 us
    all_to_all x1, blocking collectives, local(): lax.all_to_all(request, ('batch', 'item'), split_axis=0, concat_axis=0, t...  20.5 us
    all_to_all x1, waiting for transfers between devices, local(): lax.all_to_all(found, ('batch', 'item'), split_axis=0, concat_axis=0, til...  13.4 us
    all_to_all x1, waiting for transfers between devices, local(): lax.all_to_all(outgoing.reshape(devices, slots, width).astype(jnp.bfloat1...  12.5 us
    all_to_all x1, starting transfers between devices, local(): lax.all_to_all(outgoing.reshape(devices, slots, width).astype(jnp.bfloat1...  9.27 us
    scatter-add x1, other arithmetic, local(): jnp.zeros((item_table.shape[0], width), jnp.float32).at[asked.reshape(-1)]  7.29 us
    convert_element_type x1, other arithmetic, local(): return (table_grad.astype(jnp.bfloat16), weight_grad)  6 us
  transfers between devices with their start and end apart: 4, of which 4 were waited for; matrix products, arithmetic and copies ran while one was open for 7% of the time, Pallas kernels for 0%

commit v1 on v0

--- a/solution.py
+++ b/solution.py
@@ -54,14 +54,17 @@
     dhidden = (
         rscale / jnp.sqrt(jnp.float32(width)) * (dvec - hidden * rscale * rscale * inner / width)
     ).astype(jnp.bfloat16)
-    weight_grad = lax.psum_scatter(
-        lax.dot_general(
-            embed, dhidden, (((0,), (0,)), ((), ())), preferred_element_type=jnp.float32
-        ),
+    share = lax.dot_general(
+        embed, dhidden, (((0,), (0,)), ((), ())), preferred_element_type=jnp.float32
+    ).astype(jnp.bfloat16)
+    shares = lax.all_to_all(
+        share.reshape(devices, width // devices, width),
         ("batch", "item"),
-        scatter_dimension=0,
+        split_axis=0,
+        concat_axis=0,
         tiled=True,
     )
+    weight_grad = jnp.sum(shares.astype(jnp.float32), axis=0)
     drow = jnp.dot(dhidden, tower_weight.T, preferred_element_type=jnp.float32)
     outgoing = jnp.zeros((devices * slots, width), jnp.float32).at[place].set(drow)
     incoming = lax.all_to_all(

time: 246 us -> 137 us (0.56)
  waiting for transfers between devices: 158 us -> 46.8 us
  starting transfers between devices: 14 us -> 18.5 us
    unnamed x3 -> x1, waiting for transfers between devices: 111 us -> 0.02 us
    all_to_all x0 -> x1, starting transfers between devices: none -> 4.79 us  [local(): lax.all_to_all(share.reshape(devices, width // devices, width), ('batch',...]
  transfers between devices with their start and end apart: 4 -> 4, of which waited for: 4 -> 3; matrix products, arithmetic and copies ran while one was open for 7% -> 12% of each run, Pallas kernels for 0% -> 0%
where the time goes in v1:
time: 137 us; the launch traced here: 136 us
  waiting for transfers between devices  46.8 us (34%)
  blocking collectives  20.5 us (15%)
  starting transfers between devices  18.5 us (14%)
  other arithmetic  18.1 us (13%)
  between operations  14.3 us (10%)
  local copies, waits for them, and re-layouts  13.8 us (10%)
  matrix products  4.47 us (3%)
    all_gather x1, waiting for transfers between devices, local(): piece = lax.all_gather(user_unit, 'batch', axis=0, tiled=True)  21.2 us
    all_to_all x1, blocking collectives, local(): lax.all_to_all(request, ('batch', 'item'), split_axis=0, concat_axis=0, t...  20.5 us
    all_to_all x1, waiting for transfers between devices, local(): lax.all_to_all(found, ('batch', 'item'), split_axis=0, concat_axis=0, til...  13.4 us
    all_to_all x1, waiting for transfers between devices, local(): lax.all_to_all(outgoing.reshape(devices, slots, width).astype(jnp.bfloat1...  12.3 us
    all_to_all x1, starting transfers between devices, local(): lax.all_to_all(outgoing.reshape(devices, slots, width).astype(jnp.bfloat1...  9.08 us
    scatter-add x1, other arithmetic, local(): jnp.zeros((item_table.shape[0], width), jnp.float32).at[asked.reshape(-1)]  7.3 us
    convert_element_type x1, other arithmetic, local(): return (table_grad.astype(jnp.bfloat16), weight_grad)  5.93 us
    gather x2, local copies, waits for them, and re-layouts, local(): found = item_table[asked]  5.63 us
  transfers between devices with their start and end apart: 4, of which 3 were waited for; matrix products, arithmetic and copies ran while one was open for 12% of the time, Pallas kernels for 0%

profile of v1, /device:TPU:0, one launch (start us, length us, event | category | flops | bytes accessed | tf_op | source)
XLA Modules:
  0.0 136.5 jit_solution(1739416615222740926)
XLA Ops:
  7.2 0.8 copy.10
  8.0 0.2 fusion.12
  8.3 0.9 fusion.13
  9.2 0.7 compare_select_fusion.2
  9.9 1.6 %scatter_custom_fusion = s32[512]{0:T(512)S(1)} fusion(s32[256]{0:T(256)S(1)} %bitcast.38, s32[256]{0:T(256)} %param.9, s32[]{:T(128)} %constant.13.clone.1), kind=kCustom, calls=%fused_computation.45 | custom fusion | bytes 2560 | tf_op jit(solution)/shard_map/scatter | solution.py:22
  11.6 20.5 %all_to_all.27 = s32[128,1,4]{2,1,0:T(1,128)S(1)} all-to-all(s32[128,1,4]{2,1,0:T(1,128)S(1)} %bitcast.34), channel_id=1, replica_groups=mesh['batch'=8,'item'=16] {'batch','item'}, dimensions={0} | all-to-all | bytes 4096 | tf_op jit(solution)/shard_map/all_to_all | solution.py:24
  32.2 4.7 %gather_fusion = bf16[512,512]{1,0:T(8,128)(2,1)S(1)} fusion(bf16[4096,512]{1,0:T(8,128)(2,1)} %param.6, s32[1024]{0:T(1024)S(1)} %pad_clamp_fusion.1), kind=kCustom, calls=%fused_computation | custom fusion | bytes 1050624 | tf_op jit(solution)/shard_map/gather | solution.py:25
  36.9 0.9 reshape.150
  37.8 4.6 %all-to-all-start.1 = ((bf16[128,4,512]{2,1,0:T(4,128)(2,1)}), bf16[128,4,512]{2,1,0:T(4,128)(2,1)S(1)}, u32[]{:S(2)}, u32[]{:S(2)}) async-start(bf16[128,4,512]{2,1,0:T(4,128)(2,1)} %reshape.150), calls=%async_computation.1 | async-start | bytes 1048576 | tf_op jit(solution)/shard_map/all_to_all | solution.py:26
  42.5 0.1 fusion.6
  42.7 13.4 %all-to-all-done.1 = bf16[128,4,512]{2,1,0:T(4,128)(2,1)S(1)} async-done(((bf16[128,4,512]{2,1,0:T(4,128)(2,1)}), bf16[128,4,512]{2,1,0:T(4,128)(2,1)S(1)}, u32[]{:S(2)}, u32[]{:S(2)}) %all-to-all-start.1) | async-done | bytes 524320 | tf_op jit(solution)/shard_map/all_to_all | solution.py:26
  56.0 0.1 reshape.143
  56.2 1.2 gather_fusion.1
  57.3 0.4 multiply_reduce_fusion.1
  57.7 0.9 fusion.9
  58.7 21.2 %all-gather.2.cloned.1.call-done = bf16[2048,512]{1,0:T(8,128)(2,1)} async-done(((bf16[256,512]{1,0:T(8,128)(2,1)}), bf16[2048,512]{1,0:T(8,128)(2,1)}) %all-gather.2.cloned.1.call-update) | async-done | bytes 2097168 | tf_op jit(solution)/shard_map/all_gather | solution.py:38
  79.8 2.6 %fusion.19 = (f32[256]{0:T(256)S(1)}, bf16[256,2048]{1,0:T(8,128)(2,1)S(1)}) fusion(bf16[2048,512]{1,0:T(8,128)(2,1)} %all-gather.2.cloned.1.call-done, f32[256,512]{1,0:T(8,128)S(1)} %get-tuple-element.7, f32[256]{0:T(256)S(1)} %get-tuple-element.5), kind=kOutput, calls=%fused_computation.49 | convolution fusion | flops 538836736 | bytes 3672064 | tf_op jit(solution)/shard_map/dot_general | solution.py:40
  82.5 0.8 multiply_reduce_fusion
  83.3 0.2 multiply_convert_fusion
  83.5 0.3 fusion.20
  83.9 1.7 %scatter_custom_fusion.1 = f32[512,512]{1,0:T(8,128)S(1)} fusion(s32[256]{0:T(256)S(1)} %bitcast.40, f32[256,512]{1,0:T(8,128)S(1)} %fusion.20, f32[]{:T(128)} %constant.12.clone.1), kind=kCustom, calls=%fused_computation.26 | custom fusion | bytes 1048580 | tf_op jit(solution)/shard_map/scatter | solution.py:69
  85.6 0.9 convert_element_type.51
  86.5 9.1 %all-to-all-start.2 = ((bf16[128,4,512]{2,1,0:T(4,128)(2,1)}), bf16[128,4,512]{2,1,0:T(4,128)(2,1)S(1)}, u32[]{:S(2)}, u32[]{:S(2)}) async-start(bf16[128,4,512]{2,1,0:T(4,128)(2,1)} %convert_element_type.51), calls=%async_computation.2 | async-start | bytes 1048576 | tf_op jit(solution)/shard_map/all_to_all | solution.py:70
  95.6 0.3 convolution_convert_fusion
  96.0 1.0 reshape.146
  96.9 12.3 %all-to-all-done.2 = bf16[128,4,512]{2,1,0:T(4,128)(2,1)S(1)} async-done(((bf16[128,4,512]{2,1,0:T(4,128)(2,1)}), bf16[128,4,512]{2,1,0:T(4,128)(2,1)S(1)}, u32[]{:S(2)}, u32[]{:S(2)}) %all-to-all-start.2) | async-done | bytes 524320 | tf_op jit(solution)/shard_map/all_to_all | solution.py:70
  109.2 4.8 %all-to-all-start.3 = ((bf16[128,4,512]{2,1,0:T(4,128)(2,1)}), bf16[128,4,512]{2,1,0:T(4,128)(2,1)S(1)}, u32[]{:S(2)}, u32[]{:S(2)}) async-start(bf16[128,4,512]{2,1,0:T(4,128)(2,1)} %reshape.146), calls=%async_computation.3 | async-start | bytes 1048576 | tf_op jit(solution)/shard_map/all_to_all | solution.py:60
  114.0 0.5 broadcast.185
  114.5 0.8 reduce.3
  115.5 7.3 %scatter_custom_fusion.2 = f32[4096,512]{1,0:T(8,128)} fusion(s32[512]{0:T(512)S(1)} %bitcast.42, f32[512,512]{1,0:T(8,128)S(1)} %reshape.185, f32[]{:T(128)} %constant.12.clone.1), kind=kCustom, calls=%fused_computation.5 | custom fusion | flops 262144 | bytes 8388612 | tf_op jit(solution)/shard_map/scatter-add | solution.py:79
  122.8 5.9 %convert_element_type.52 = bf16[4096,512]{1,0:T(8,128)(2,1)} convert(f32[4096,512]{1,0:T(8,128)} %scatter_custom_fusion.2) | non-fusion elementwise | flops 2097152 | bytes 12582912 | tf_op jit(solution)/shard_map/convert_element_type | solution.py:81
  128.8 0.9 convert_reduce_fusion
  (29 shorter events, 0.7 us)
Async XLA Ops:
  7.2 50.2 %copy-start = (bf16[512,512]{1,0:T(8,128)(2,1)S(1)}, bf16[512,512]{1,0:T(8,128)(2,1)}, u32[]{:S(2)}) copy-start(bf16[512,512]{1,0:T(8,128)(2,1)} %param.7) | copy-start | bytes 1572868
  36.9 5.6 %copy-start.1 = (bf16[256,512]{1,0:T(8,128)(2,1)S(1)}, bf16[256,512]{1,0:T(8,128)(2,1)}, u32[]{:S(2)}) copy-start(bf16[256,512]{1,0:T(8,128)(2,1)} %param.5) | copy-start | bytes 786436
  37.8 18.2 %all-to-all-start.1 = ((bf16[128,4,512]{2,1,0:T(4,128)(2,1)}), bf16[128,4,512]{2,1,0:T(4,128)(2,1)S(1)}, u32[]{:S(2)}, u32[]{:S(2)}) async-start(bf16[128,4,512]{2,1,0:T(4,128)(2,1)} %reshape.150), calls=%async_computation.1 | async-start | bytes 1048576 | tf_op jit(solution)/shard_map/all_to_all | solution.py:26
  42.5 37.4 %all-gather.2.cloned.1.call-start = ((), (), s32[]{:S(2)}) async-start(), calls=%async_computation.4 | async-start | bytes 2359296 | tf_op jit(solution)/shard_map/all_gather | solution.py:38
  58.7 23.8 %copy-start.2 = (bf16[256,512]{1,0:T(8,128)(2,1)S(1)}, bf16[256,512]{1,0:T(8,128)(2,1)}, u32[]{:S(2)}) copy-start(bf16[256,512]{1,0:T(8,128)(2,1)} %get-tuple-element.3) | copy-start | bytes 786436
  79.8 2.6 %copy-start.3 = (bf16[2048,512]{1,0:T(8,128)(2,1)S(1)}, bf16[2048,512]{1,0:T(8,128)(2,1)}, u32[]{:S(2)}) copy-start(bf16[2048,512]{1,0:T(8,128)(2,1)} %all-gather.2.cloned.1.call-done) | copy-start | bytes 6291460
  86.5 22.7 %all-to-all-start.2 = ((bf16[128,4,512]{2,1,0:T(4,128)(2,1)}), bf16[128,4,512]{2,1,0:T(4,128)(2,1)S(1)}, u32[]{:S(2)}, u32[]{:S(2)}) async-start(bf16[128,4,512]{2,1,0:T(4,128)(2,1)} %convert_element_type.51), calls=%async_computation.2 | async-start | bytes 1048576 | tf_op jit(solution)/shard_map/all_to_all | solution.py:70
  109.2 19.6 %all-to-all-start.3 = ((bf16[128,4,512]{2,1,0:T(4,128)(2,1)}), bf16[128,4,512]{2,1,0:T(4,128)(2,1)S(1)}, u32[]{:S(2)}, u32[]{:S(2)}) async-start(bf16[128,4,512]{2,1,0:T(4,128)(2,1)} %reshape.146), calls=%async_computation.3 | async-start | bytes 1048576 | tf_op jit(solution)/shard_map/all_to_all | solution.py:60
Sparse Core Ops, SparseCore 0:
  58.8 21.0 all-gather.1

commit v2 on v0

v2 whole, which is shorter than its diff:
```python
import functools

import jax
import jax.numpy as jnp
from jax import lax
from jax.experimental import pallas as pl
from jax.experimental.pallas import tpu as pltpu
from jax.sharding import PartitionSpec as P

epsilon = 1e-06
score_scale = 60.0
cauchy_scale = 4.0

MESH = pl.DeviceIdType.MESH
BF = jnp.bfloat16
F32 = jnp.float32
I32 = jnp.int32
D = 512
BD = 256
ROWS = 4096
SLOTS = 4
NDEV = 128
NCH = 4
CH = NDEV // NCH
CS = CH * SLOTS


def nt(a, b):
    return lax.dot_general(a, b, (((1,), (1,)), ((), ())), preferred_element_type=F32)


def tn(a, b):
    return lax.dot_general(a, b, (((0,), (0,)), ((), ())), preferred_element_type=F32)


def step_kernel(
    user_ref,
    table_ref,
    w_ref,
    owner_ref,
    row_ref,
    drow_out,
    askrow_out,
    wg_out,
    table_v,
    req,
    t1,
    asked,
    cols,
    reply,
    emb,
    embn,
    drs,
    dr,
    ug,
    us,
    valid,
    dhid,
    onehot,
    wgs,
    wgr,
    wg2,
    wg3,
    tsem,
    ag_s,
    ag_r,
    rq_s,
    rq_r,
    rp_s,
    rp_r,
    gr_s,
    gr_r,
    wg_s,
    wg_r,
):
    b, it = lax.axis_index("batch"), lax.axis_index("item")
    x, c = b // 2, lax.rem(b, 2)
    z, y = it // 4, lax.rem(it, 4)

    def at(xi, ga, ze, et):
        px, pc = lax.rem(x + xi, 4), lax.rem(c + ga, 2)
        pz, py = lax.rem(z + ze, 4), lax.rem(y + et, 4)
        return (px * 2 + pc, pz * 4 + py)

    def send(src, dst, ss, rs, to):
        cp = pltpu.make_async_remote_copy(
            src_ref=src, dst_ref=dst, send_sem=ss, recv_sem=rs, device_id=to, device_id_type=MESH
        )
        cp.start()

    def drain(ref, sem):
        pltpu.make_async_copy(ref, ref, sem).wait()

    table_cp = pltpu.make_async_copy(table_ref, table_v, tsem)
    table_cp.start()

    bar = pltpu.get_barrier_semaphore()
    for k in range(1, 8):
        pl.semaphore_signal(bar, inc=1, device_id=at(k // 2, k % 2, 0, 0), device_id_type=MESH)
    for k in range(1, 16):
        pl.semaphore_signal(bar, inc=1, device_id=at(0, 0, k // 4, k % 4), device_id_type=MESH)

    uf = user_ref[...].astype(F32)
    uu = (
        uf
        * lax.rsqrt(jnp.mean(uf * uf, axis=1, keepdims=True) + epsilon)
        / jnp.sqrt(F32(D))
    ).astype(BF)
    ug[0] = uu

    ow = owner_ref[...]
    ox, oc = ow // 32, (ow // 16) % 2
    oz, oy = (ow // 4) % 4, ow % 4
    rx, rc = (ox - x + 4) % 4, (oc - c + 2) % 2
    rz, ry = (oz - z + 4) % 4, (oy - y + 4) % 4
    pos = (ry * 8 + rx * 2 + rc) * 4 + rz
    oh = pos == lax.broadcasted_iota(I32, (NDEV, BD), 0)
    ohf = jnp.where(oh, F32(1), F32(0))
    upper = jnp.where(
        lax.broadcasted_iota(I32, (BD, BD), 0) < lax.broadcasted_iota(I32, (BD, BD), 1),
        F32(1),
        F32(0),
    ).astype(BF)
    before = jnp.dot(ohf.astype(BF), upper, preferred_element_type=F32)
    rank = jnp.sum(before * ohf, axis=0, keepdims=True)
    place = pos * SLOTS + rank.astype(I32)
    pt = place == lax.broadcasted_iota(I32, (NDEV * SLOTS, BD), 0)
    ptf = jnp.where(pt, F32(1), F32(0))
    want = jnp.sum(jnp.where(pt, row_ref[...].astype(F32), F32(0)), axis=1, keepdims=True)
    req[...] = jnp.broadcast_to(want.astype(I32), (NDEV * SLOTS, 128)).reshape(
        NCH, 8, 4, SLOTS, 128
    )
    valid[...] = jnp.broadcast_to(jnp.sum(ptf, axis=1, keepdims=True), (NDEV * SLOTS, 128))

    pl.semaphore_wait(bar, 22)

    for k in range(1, 8):
        send(req.at[:, k], t1.at[:, k], rq_s.at[0], rq_r.at[0], at(k // 2, k % 2, 0, 0))
    send(ug.at[0], ug.at[1], ag_s.at[0], ag_r.at[0], at(0, 1, 0, 0))
    send(ug.at[0], ug.at[2], ag_s.at[1], ag_r.at[1], at(1, 0, 0, 0))
    send(ug.at[0], ug.at[4], ag_s.at[2], ag_r.at[2], at(3, 0, 0, 0))
    t1[:, 0] = req[:, 0]
    us[...] = jnp.dot(ptf.astype(BF), ug[0], preferred_element_type=F32).astype(BF)
    drain(t1.at[:, pl.ds(1, 7)], rq_r.at[0])
    for k in range(1, 16):
        ze, et = k // 4, k % 4
        send(t1.at[et, :, ze], asked.at[et, :, ze], rq_s.at[1], rq_r.at[1], at(0, 0, ze, et))
    asked[0, :, 0] = t1[0, :, 0]
    table_cp.wait()
    drain(req.at[:, pl.ds(1, 7)], rq_s.at[0])
    h = BD // 2
    drain(ug.at[2], ag_r.at[1])
    send(ug.at[2, pl.ds(0, h)], ug.at[6, pl.ds(0, h)], ag_s.at[3], ag_r.at[3], at(1, 0, 0, 0))
    send(ug.at[2], ug.at[3], ag_s.at[5], ag_r.at[5], at(0, 1, 0, 0))
    drain(ug.at[4], ag_r.at[2])
    send(ug.at[4, pl.ds(h, h)], ug.at[6, pl.ds(h, h)], ag_s.at[4], ag_r.at[4], at(3, 0, 0, 0))
    send(ug.at[4], ug.at[5], ag_s.at[6], ag_r.at[6], at(0, 1, 0, 0))

    hop2 = cols.at[pl.ds(0, 15 * 8 * SLOTS)]
    drain(hop2, rq_r.at[1])

    cols[...] = asked[...].reshape(NDEV * SLOTS, 128)
    eye = lax.broadcasted_iota(I32, (128, 128), 0) == lax.broadcasted_iota(I32, (128, 128), 1)
    for g in range(NCH):
        a = cols[g * CS : (g + 1) * CS, :]
        askrow_out[:, g * CS : (g + 1) * CS] = jnp.broadcast_to(
            jnp.sum(jnp.where(eye, a, 0), axis=0, keepdims=True), (8, CS)
        )
        for j in range(ROWS // 128):
            hit = a == lax.broadcasted_iota(I32, (CS, 128), 1) + j * 128
            onehot[g * CS : (g + 1) * CS, j * 128 : (j + 1) * 128] = jnp.where(
                hit, F32(1), F32(0)
            ).astype(BF)
        found = jnp.dot(
            onehot[g * CS : (g + 1) * CS, :], table_v[...], preferred_element_type=F32
        )
        reply[g * CH : (g + 1) * CH] = found.astype(BF).reshape(CH, SLOTS, D)

        def back(i, _):
            beta, ze = lax.rem(i // 4, 8), lax.rem(i, 4)
            to = at(4 - beta // 2, lax.rem(beta, 2), 4 - ze, 4 - g)
            send(reply.at[pl.ds(i, 1)], emb.at[pl.ds(i, 1)], rp_s, rp_r.at[g], to)
            return 0

        lax.fori_loop(max(1, g * CH), (g + 1) * CH, back, 0)
        if g == 0:
            emb[0] = reply[0]

    drain(ug.at[6, pl.ds(0, h)], ag_r.at[3])
    drain(ug.at[6, pl.ds(h, h)], ag_r.at[4])
    send(ug.at[6], ug.at[7], ag_s.at[7], ag_r.at[7], at(0, 1, 0, 0))
    drain(ug.at[1], ag_r.at[0])
    drain(ug.at[3], ag_r.at[5])
    drain(ug.at[5], ag_r.at[6])
    drain(ug.at[7], ag_r.at[7])
    root = jnp.sqrt(F32(D))
    for g in range(NCH):
        lo = 1 if g == 0 else g * CH
        drain(emb.at[pl.ds(lo, (g + 1) * CH - lo)], rp_r.at[g])
        sl = slice(g * CS, (g + 1) * CS)
        e = emb[g * CH : (g + 1) * CH].reshape(CS, D)
        embn[sl, :] = e
        hid = jnp.dot(e, w_ref[...], preferred_element_type=F32)
        rs = lax.rsqrt(jnp.mean(hid * hid, axis=1, keepdims=True) + epsilon)
        iv = (hid * rs / root).astype(BF)
        tot = jnp.zeros((CS, 1), F32)
        mix = jnp.zeros((CS, D), F32)
        for k in range(8):
            ex = jnp.exp(nt(iv, ug[k]) * score_scale)
            tot = tot + jnp.sum(ex, axis=1, keepdims=True)
            mix = mix + jnp.dot(ex.astype(BF), ug[k], preferred_element_type=F32)
        uf2 = us[sl, :].astype(F32)
        positive = jnp.sum(iv.astype(F32) * uf2, axis=1, keepdims=True) * score_scale
        xent = jnp.log(tot) - positive
        cw = 1.0 / (1.0 + xent / cauchy_scale)
        dvec = cw * score_scale * (mix / tot - uf2)
        inner = jnp.sum(hid * dvec, axis=1, keepdims=True)
        dh = rs / root * (dvec - hid * rs * rs * inner / D)
        dh = jnp.where(valid[sl, 0:1] > 0.5, dh, F32(0)).astype(BF)
        dhid[sl, :] = dh
        drs[g * CH : (g + 1) * CH] = nt(dh, w_ref[...]).astype(BF).reshape(CH, SLOTS, D)

        def out(i, _):
            beta, ze = lax.rem(i // 4, 8), lax.rem(i, 4)
            to = at(beta // 2, lax.rem(beta, 2), ze, g)
            send(drs.at[pl.ds(i, 1)], dr.at[pl.ds(i, 1)], gr_s, gr_r, to)
            return 0

        lax.fori_loop(lo, (g + 1) * CH, out, 0)
    dr[0] = drs[0]

    wgs[...] = tn(embn[...], dhid[...]).astype(BF).reshape(8, 64, D)
    for k in range(4):
        send(wgs.at[k * 2 + 1 - c], wgr.at[k], wg_s.at[0], wg_r.at[0], at(0, 1, 0, 0))
    drain(wgr, wg_r.at[0])
    for k in range(4):
        both = wgs[k * 2 + c].astype(F32) + wgr[k].astype(F32)
        wg2[k * 16 : (k + 1) * 16] = both.astype(BF).reshape(16, 4, D)

    def spread(j, _):
        xi, ze, et = j // 16, lax.rem(j // 4, 4), lax.rem(j, 4)
        to = at(xi, 0, ze, et)
        mine = lax.rem(x + xi, 4) * 16 + lax.rem(z + ze, 4) * 4 + lax.rem(y + et, 4)
        send(wg2.at[pl.ds(mine, 1)], wg3.at[pl.ds(j, 1)], wg_s.at[1], wg_r.at[1], to)
        return 0

    lax.fori_loop(1, 64, spread, 0)
    wg3[0] = wg2[x * 16 + z * 4 + y]

    drain(dr.at[pl.ds(1, NDEV - 1)], gr_r)
    drow_out[...] = dr[...].reshape(NDEV * SLOTS, D)

    drain(wg3.at[pl.ds(1, 63)], wg_r.at[1])
    wg_out[...] = jnp.sum(wg3[...].astype(F32), axis=0)

    drain(hop2, rq_s.at[1])
    for k in range(3):
        drain(ug.at[0], ag_s.at[k])
    drain(ug.at[2, pl.ds(0, h)], ag_s.at[3])
    drain(ug.at[4, pl.ds(h, h)], ag_s.at[4])
    drain(ug.at[2], ag_s.at[5])
    drain(ug.at[4], ag_s.at[6])
    drain(ug.at[6], ag_s.at[7])
    drain(reply.at[pl.ds(1, NDEV - 1)], rp_s)
    drain(drs.at[pl.ds(1, NDEV - 1)], gr_s)
    drain(wgr, wg_s.at[0])
    drain(wg2.at[pl.ds(1, 63)], wg_s.at[1])


def table_kernel(ask_ref, drow_ref, out_ref):
    n = out_ref.shape[0]
    base = pl.program_id(0) * n
    hit = ask_ref[0:1, :] == lax.broadcasted_iota(I32, (n, NDEV * SLOTS), 0) + base
    mat = jnp.where(hit, F32(1), F32(0)).astype(BF)
    out_ref[...] = jnp.dot(mat, drow_ref[...], preferred_element_type=F32).astype(BF)


def local(user_vectors, item_table, tower_weight, item_owner, item_row):
    dma = pltpu.SemaphoreType.DMA
    vm = pl.BlockSpec(memory_space=pltpu.VMEM)
    n = NDEV * SLOTS
    scratch = [
        pltpu.VMEM((ROWS, D), BF),
        pltpu.VMEM((4, 8, 4, SLOTS, 128), I32),
        pltpu.VMEM((4, 8, 4, SLOTS, 128), I32),
        pltpu.VMEM((4, 8, 4, SLOTS, 128), I32),
        pltpu.VMEM((n, 128), I32),
        pltpu.VMEM((NDEV, SLOTS, D), BF),
        pltpu.VMEM((NDEV, SLOTS, D), BF),
        pltpu.VMEM((n, D), BF),
        pltpu.VMEM((NDEV, SLOTS, D), BF),
        pltpu.VMEM((NDEV, SLOTS, D), BF),
        pltpu.VMEM((8, BD, D), BF),
        pltpu.VMEM((n, D), BF),
        pltpu.VMEM((n, 128), F32),
        pltpu.VMEM((n, D), BF),
        pltpu.VMEM((n, ROWS), BF),
        pltpu.VMEM((8, 64, D), BF),
        pltpu.VMEM((4, 64, D), BF),
        pltpu.VMEM((64, 4, D), BF),
        pltpu.VMEM((64, 4, D), BF),
        dma,
        dma((8,)),
        dma((8,)),
        dma((2,)),
        dma((2,)),
        dma,
        dma((NCH,)),
        dma,
        dma,
        dma((2,)),
        dma((2,)),
    ]
    drow, ask, wgrad = pl.pallas_call(
        step_kernel,
        out_shape=(
            jax.ShapeDtypeStruct((n, D), BF),
            jax.ShapeDtypeStruct((8, n), I32),
            jax.ShapeDtypeStruct((4, D), F32),
        ),
        in_specs=[vm, pl.BlockSpec(memory_space=pl.ANY), vm, vm, vm],
        out_specs=(vm, vm, vm),
        scratch_shapes=scratch,
        compiler_params=pltpu.CompilerParams(
            collective_id=0, has_side_effects=True, vmem_limit_bytes=60 * 1024 * 1024
        ),
    )(user_vectors, item_table, tower_weight, item_owner.reshape(1, BD), item_row.reshape(1, BD))
    blk = 512
    tgrad = pl.pallas_call(
        table_kernel,
        grid=(ROWS // blk,),
        out_shape=jax.ShapeDtypeStruct((ROWS, D), BF),
        in_specs=[
            pl.BlockSpec((8, n), lambda i: (0, 0)),
            pl.BlockSpec((n, D), lambda i: (0, 0)),
        ],
        out_specs=pl.BlockSpec((blk, D), lambda i: (i, 0)),
    )(ask, drow)
    return tgrad, wgrad


def solution(mesh):
    return jax.shard_map(
        local,
        mesh=mesh,
        in_specs=(
            P(("batch", "item"), None),
            P(("batch", "item"), None),
            P(),
            P(("batch", "item"), None),
            P(("batch", "item")),
        ),
        out_specs=(P(("batch", "item"), None), P(("batch", "item"), None)),
        check_vma=False,
    )
```

time: 246 us -> 62.8 us (0.26)
  waiting for transfers between devices: 158 us -> 0 us
  Pallas kernels: 0 us -> 61.4 us
  blocking collectives: 20.5 us -> 0 us
  other arithmetic: 17.2 us -> 0 us
  starting transfers between devices: 14 us -> 0 us
  between operations: 14.3 us -> 0.65 us
  local copies, waits for them, and re-layouts: 14.2 us -> 0.6 us
  matrix products: 5.44 us -> 0 us
    unnamed x3 -> x0, waiting for transfers between devices: 111 us -> none
    pallas_call x0 -> x2, Pallas kernels: none -> 61.4 us  [the longest x1 55 us: local(): pl.pallas_call(step_kernel, out_shape=(jax.ShapeDtypeStruct((n, D), BF),...]
    all_to_all x2 -> x0, waiting for transfers between devices: 25.9 us -> none  [the longest x1 13.4 us: local(): lax.all_to_all(found, ('batch', 'item'), split_axis=0, concat_axis=0, til...]
    all_gather x1 -> x0, waiting for transfers between devices: 21.1 us -> none  [local(): piece = lax.all_gather(user_unit, 'batch', axis=0, tiled=True)]
    all_to_all x1 -> x0, blocking collectives: 20.5 us -> none  [local(): lax.all_to_all(request, ('batch', 'item'), split_axis=0, concat_axis=0, t...]
    all_to_all x2 -> x0, starting transfers between devices: 13.9 us -> none  [the longest x1 9.27 us: local(): lax.all_to_all(outgoing.reshape(devices, slots, width).astype(jnp.bfloat1...]
    scatter-add x1 -> x0, other arithmetic: 7.29 us -> none  [local(): jnp.zeros((item_table.shape[0], width), jnp.float32).at[asked.reshape(-1)]]
    gather x3 -> x0, local copies, waits for them, and re-layouts: 6.78 us -> none  [the longest x2 5.63 us: local(): found = item_table[asked]]
  transfers between devices with their start and end apart: 4 -> 0, of which waited for: 4 -> 0; matrix products, arithmetic and copies ran while one was open for 7% -> 0% of each run, Pallas kernels for 0% -> 0%
where the time goes in v2:
time: 62.8 us; the launch traced here: 62.7 us
  Pallas kernels  61.4 us (98%)
  between operations  0.65 us (1%)
    pallas_call x1, Pallas kernels, local(): pl.pallas_call(step_kernel, out_shape=(jax.ShapeDtypeStruct((n, D), BF),...  55 us
    pallas_call x1, Pallas kernels, local(): pl.pallas_call(table_kernel, grid=(ROWS // blk,), out_shape=jax.ShapeDtyp...  6.49 us

profile of v2, /device:TPU:0, one launch (start us, length us, event | category | flops | bytes accessed | tf_op | source)
XLA Modules:
  0.0 62.7 jit_solution(1959592893697790346)
XLA Ops:
  0.6 55.0 %shard_map.68 = (bf16[512,512]{1,0:T(8,128)(2,1)}, s32[8,512]{1,0:T(8,128)}, f32[4,512]{1,0:T(4,128)}) custom-call(bf16[256,512]{1,0:T(8,128)(2,1)} %user_ref.1, bf16[4096,512]{1,0:T(8,128)(2,1)} %table_ref.1, bf16[512,512]{1,0:T(8,128)(2,1)} %w_ref.1, s32[1,256]{1,0:T(1,128)} %bitcast.2, s32[1,256]{1,0:T(1,128)} %bitcast.3), custom_call_target="tpu_custom_call" | custom-call | tf_op jit(solution)/shard_map/pallas_call | solution.py:314
  55.6 0.0 copy-start
  55.6 6.5 %shard_map.69 = bf16[4096,512]{1,0:T(8,128)(2,1)} custom-call(s32[8,512]{1,0:T(8,128)} %get-tuple-element.5.ask_ref, bf16[512,512]{1,0:T(8,128)(2,1)} %get-tuple-element.6.drow_ref), custom_call_target="tpu_custom_call" | custom-call | tf_op jit(solution)/shard_map/pallas_call | solution.py:329
  62.1 0.0 copy-done
  62.1 0.6 copy.8
Async XLA Ops:
  55.6 6.5 %copy-start = (f32[4,512]{1,0:T(4,128)S(1)}, f32[4,512]{1,0:T(4,128)}, u32[]{:S(2)}) copy-start(f32[4,512]{1,0:T(4,128)} %get-tuple-element.11) | copy-start | bytes 24580

commit v3 on v2

v3 whole, which is shorter than its diff:
```python
import functools

import jax
import jax.numpy as jnp
from jax import lax
from jax.experimental import pallas as pl
from jax.experimental.pallas import tpu as pltpu
from jax.sharding import PartitionSpec as P

epsilon = 1e-06
score_scale = 60.0
cauchy_scale = 4.0

MESH = pl.DeviceIdType.MESH
BF = jnp.bfloat16
F32 = jnp.float32
I32 = jnp.int32
D = 512
BD = 256
ROWS = 4096
SLOTS = 4
NDEV = 128
NCH = 4
CH = NDEV // NCH
CS = CH * SLOTS


def nt(a, b):
    return lax.dot_general(a, b, (((1,), (1,)), ((), ())), preferred_element_type=F32)


def tn(a, b):
    return lax.dot_general(a, b, (((0,), (0,)), ((), ())), preferred_element_type=F32)


def step_kernel(
    user_ref,
    table_ref,
    w_ref,
    owner_ref,
    row_ref,
    drow_out,
    askrow_out,
    wg_out,
    user_v,
    w_v,
    owner_v,
    row_v,
    table_v,
    req,
    t1,
    asked,
    cols,
    reply,
    emb,
    drs,
    dr,
    ug,
    back,
    forth,
    exb,
    onehot,
    wgs,
    wgr,
    wg2,
    wg3,
    in_s,
    ag_s,
    ag_r,
    rq_s,
    rq_r,
    rp_s,
    rp_r,
    gr_s,
    gr_r,
    wg_s,
    wg_r,
):
    b, it = lax.axis_index("batch"), lax.axis_index("item")
    x, c = b // 2, lax.rem(b, 2)
    z, y = it // 4, lax.rem(it, 4)
    xs = [lax.rem(x + k, 4) * 2 for k in range(4)]
    cs = [lax.rem(c + k, 2) for k in range(2)]
    zs = [lax.rem(z + k, 4) * 4 for k in range(4)]
    ys = [lax.rem(y + k, 4) for k in range(4)]

    def at(xi, ga, ze, et):
        return (xs[xi % 4] + cs[ga % 2], zs[ze % 4] + ys[et % 4])

    def split(i):
        return (i % 8) // 2, i % 2, (i // 8) % 4, i // 32

    def send(src, dst, ss, rs, to):
        pltpu.make_async_remote_copy(
            src_ref=src, dst_ref=dst, send_sem=ss, recv_sem=rs, device_id=to, device_id_type=MESH
        ).start()

    def drain(ref, sem):
        pltpu.make_async_copy(ref, ref, sem).wait()

    fetch = [
        pltpu.make_async_copy(src, dst, in_s.at[k])
        for k, (src, dst) in enumerate(
            [
                (owner_ref, owner_v),
                (row_ref, row_v),
                (user_ref, user_v),
                (w_ref, w_v),
                (table_ref, table_v),
            ]
        )
    ]
    for cp in fetch:
        cp.start()
    bar = pltpu.get_barrier_semaphore()
    for k in range(1, 8):
        pl.semaphore_signal(bar, inc=1, device_id=at(k // 2, k % 2, 0, 0), device_id_type=MESH)
    for k in range(1, 16):
        pl.semaphore_signal(bar, inc=1, device_id=at(0, 0, k % 4, k // 4), device_id_type=MESH)

    fetch[0].wait()
    fetch[1].wait()
    ow = owner_v[...]
    ox, oc = ow // 32, (ow // 16) % 2
    oz, oy = (ow // 4) % 4, ow % 4
    rx, rc = (ox - x + 4) % 4, (oc - c + 2) % 2
    rz, ry = (oz - z + 4) % 4, (oy - y + 4) % 4
    beta = rx * 2 + rc
    plane = ry * 4 + rz
    pos = plane * 8 + beta
    ohf = jnp.where(pos == lax.broadcasted_iota(I32, (NDEV, BD), 0), F32(1), F32(0))
    upper = jnp.where(
        lax.broadcasted_iota(I32, (BD, BD), 0) < lax.broadcasted_iota(I32, (BD, BD), 1),
        F32(1),
        F32(0),
    ).astype(BF)
    before = jnp.dot(ohf.astype(BF), upper, preferred_element_type=F32)
    rank = jnp.sum(before * ohf, axis=0, keepdims=True).astype(I32)
    rw = row_v[...]
    here = beta == lax.broadcasted_iota(I32, (8, BD), 0)
    high = jnp.where(here, (rw // 64).astype(F32), F32(0)).astype(BF)
    low = jnp.where(here, (rw % 64).astype(F32), F32(0)).astype(BF)
    lane = plane * SLOTS + rank
    spot = jnp.where(
        lane == lax.broadcasted_iota(I32, (128, BD), 0), F32(1), F32(0)
    ).astype(BF)
    want = nt(high, spot) * 64.0 + nt(low, spot)
    req[...] = want.astype(I32).reshape(8, 1, 128)

    pl.semaphore_wait(bar, 22)
    for k in range(1, 8):
        send(req.at[k], t1.at[k], rq_s.at[0], rq_r.at[0], at(k // 2, k % 2, 0, 0))
    t1[0] = req[0]

    fetch[2].wait()
    uf = user_v[...].astype(F32)
    uu = (
        uf
        * lax.rsqrt(jnp.mean(uf * uf, axis=1, keepdims=True) + epsilon)
        / jnp.sqrt(F32(D))
    ).astype(BF)
    ug[0] = uu
    h = BD // 2
    top, bot = pl.ds(0, h), pl.ds(h, h)
    right, left, other = at(1, 0, 0, 0), at(3, 0, 0, 0), at(0, 1, 0, 0)

    def share(m, src, dst, to):
        send(src, dst, ag_s.at[m], ag_r.at[m], to)

    share(1, ug.at[0, top], ug.at[2, top], right)
    share(3, ug.at[0, bot], ug.at[4, bot], left)
    share(2, ug.at[0, bot], ug.at[2, bot], right)
    share(4, ug.at[0, top], ug.at[4, top], left)
    share(0, ug.at[0], ug.at[1], other)

    drain(t1.at[pl.ds(1, 7)], rq_r.at[0])
    for k in range(1, 16):
        send(t1, asked.at[k], rq_s.at[1], rq_r.at[1], at(0, 0, k % 4, k // 4))
    asked[0] = t1[...]

    place = pos * SLOTS + rank
    forth[...] = jnp.where(
        place == lax.broadcasted_iota(I32, (NDEV * SLOTS, BD), 0), F32(1), F32(0)
    ).astype(BF)
    diag = lax.broadcasted_iota(I32, (BD, BD), 0) == lax.broadcasted_iota(I32, (BD, BD), 1)
    down = jnp.sum(jnp.where(diag, place.astype(F32), F32(0)), axis=1, keepdims=True).astype(I32)
    back[...] = jnp.where(
        down == lax.broadcasted_iota(I32, (BD, NDEV * SLOTS), 1), F32(1), F32(0)
    ).astype(BF)
    rowq = lax.broadcasted_iota(I32, (NDEV * SLOTS, 128), 0)
    lanq = lax.broadcasted_iota(I32, (NDEV * SLOTS, 128), 1)
    grow = jnp.where(rowq // SLOTS == lanq, F32(1), F32(0)).astype(BF)
    ones = jnp.ones((128, 128), BF)
    fetch[4].wait()

    drain(asked.at[pl.ds(1, 15)], rq_r.at[1])
    parts = []
    for k in range(16):
        a = asked[k].reshape(8, 128)
        parts.append(pltpu.roll(a, (128 - 4 * k) % 128, 1) if k else a)
    flat = jnp.concatenate(parts, axis=0)
    hi = jnp.dot(grow, (flat // 64).astype(F32).astype(BF), preferred_element_type=F32)
    lo = jnp.dot(grow, (flat % 64).astype(F32).astype(BF), preferred_element_type=F32)
    mine = lanq == rowq % SLOTS
    picked = jnp.where(mine, hi * 64.0, F32(0)).astype(BF)
    picked2 = jnp.where(mine, lo, F32(0)).astype(BF)
    cols[...] = (
        jnp.dot(picked, ones, preferred_element_type=F32)
        + jnp.dot(picked2, ones, preferred_element_type=F32)
    ).astype(I32)

    for g in range(NCH):
        a = cols[g * CS : (g + 1) * CS, :]
        for j in range(ROWS // 128):
            hit = a == lax.broadcasted_iota(I32, (CS, 128), 1) + j * 128
            onehot[g * CS : (g + 1) * CS, j * 128 : (j + 1) * 128] = jnp.where(
                hit, F32(1), F32(0)
            ).astype(BF)
        found = jnp.dot(
            onehot[g * CS : (g + 1) * CS, :], table_v[...], preferred_element_type=F32
        )
        reply[g * CH : (g + 1) * CH] = found.astype(BF).reshape(CH, SLOTS, D)
        for i in range(max(1, g * CH), (g + 1) * CH):
            xi, ga, ze, et = split(i)
            to = at(4 - xi, ga, 4 - ze, 4 - et)
            send(reply.at[i], emb.at[i], rp_s, rp_r, to)
        if g == 0:
            drain(ug.at[2, top], ag_r.at[1])
            share(5, ug.at[2, top], ug.at[6, top], right)
            drain(ug.at[4, bot], ag_r.at[3])
            share(6, ug.at[4, bot], ug.at[6, bot], left)
        if g == 1:
            drain(ug.at[2, bot], ag_r.at[2])
            share(7, ug.at[2], ug.at[3], other)
            drain(ug.at[4, top], ag_r.at[4])
            share(8, ug.at[4], ug.at[5], other)
    emb[0] = reply[0]
    eye = lax.broadcasted_iota(I32, (128, 128), 0) == lax.broadcasted_iota(I32, (128, 128), 1)
    for g in range(NCH):
        a = cols[g * CS : (g + 1) * CS, :]
        askrow_out[:, g * CS : (g + 1) * CS] = jnp.broadcast_to(
            jnp.sum(jnp.where(eye, a, 0), axis=0, keepdims=True), (8, CS)
        )

    drain(ug.at[6, top], ag_r.at[5])
    share(9, ug.at[6, top], ug.at[7, top], other)
    drain(ug.at[6, bot], ag_r.at[6])
    share(10, ug.at[6, bot], ug.at[7, bot], other)
    drain(ug.at[1], ag_r.at[0])
    drain(ug.at[3], ag_r.at[7])
    drain(ug.at[5], ag_r.at[8])
    fetch[3].wait()

    drain(emb.at[pl.ds(1, NDEV - 1)], rp_r)
    e = jnp.dot(
        back[...], emb[...].reshape(NDEV * SLOTS, D), preferred_element_type=F32
    ).astype(BF)
    root = jnp.sqrt(F32(D))
    hid = jnp.dot(e, w_v[...], preferred_element_type=F32)
    rs = lax.rsqrt(jnp.mean(hid * hid, axis=1, keepdims=True) + epsilon)
    iv = (hid * rs / root).astype(BF)
    uf2 = ug[0].astype(F32)
    positive = jnp.sum(iv.astype(F32) * uf2, axis=1, keepdims=True) * score_scale
    drain(ug.at[7, top], ag_r.at[9])
    drain(ug.at[7, bot], ag_r.at[10])
    tot = jnp.zeros((BD, 1), F32)
    for k in range(8):
        ex = jnp.exp(nt(iv, ug[k]) * score_scale)
        tot = tot + jnp.sum(ex, axis=1, keepdims=True)
        exb[:, k * BD : (k + 1) * BD] = ex.astype(BF)
    mix = jnp.dot(exb[...], ug[...].reshape(8 * BD, D), preferred_element_type=F32)
    xent = jnp.log(tot) - positive
    cw = 1.0 / (1.0 + xent / cauchy_scale)
    dvec = cw * score_scale * (mix / tot - uf2)
    inner = jnp.sum(hid * dvec, axis=1, keepdims=True)
    dh = (rs / root * (dvec - hid * rs * rs * inner / D)).astype(BF)

    wgs[...] = tn(e, dh).astype(BF).reshape(8, 64, D)
    for k in range(4):
        send(wgs.at[k * 2 + 1 - c], wgr.at[k], wg_s.at[0], wg_r.at[0], other)

    drow = nt(dh, w_v[...]).astype(BF)
    for g in range(NCH):
        part = jnp.dot(forth[g * CS : (g + 1) * CS, :], drow, preferred_element_type=F32)
        drs[g * CH : (g + 1) * CH] = part.astype(BF).reshape(CH, SLOTS, D)
        for i in range(max(1, g * CH), (g + 1) * CH):
            send(drs.at[i], dr.at[i], gr_s, gr_r, at(*split(i)))
    dr[0] = drs[0]

    drain(wgr, wg_r.at[0])
    for k in range(4):
        both = wgs[k * 2 + c].astype(F32) + wgr[k].astype(F32)
        wg2[k * 16 : (k + 1) * 16] = both.astype(BF).reshape(16, 4, D)
    for j in range(1, 64):
        xi, ze, et = j // 16, (j // 4) % 4, j % 4
        src = wg2.at[xs[xi] * 8 + zs[ze] + ys[et]]
        send(src, wg3.at[j], wg_s.at[1], wg_r.at[1], at(xi, 0, ze, et))
    wg3[0] = wg2[x * 16 + z * 4 + y]

    drain(dr.at[pl.ds(1, NDEV - 1)], gr_r)
    drow_out[...] = dr[...].reshape(NDEV * SLOTS, D)
    drain(wg3.at[pl.ds(1, 63)], wg_r.at[1])
    wg_out[...] = jnp.sum(wg3[...].astype(F32), axis=0)

    drain(t1.at[pl.ds(1, 7)], rq_s.at[0])
    drain(asked.at[pl.ds(1, 15)], rq_s.at[1])
    drain(ug.at[0], ag_s.at[0])
    for m in (1, 2, 3, 4, 5, 6, 9, 10):
        drain(ug.at[0, top], ag_s.at[m])
    for m in (7, 8):
        drain(ug.at[0], ag_s.at[m])
    drain(reply.at[pl.ds(1, NDEV - 1)], rp_s)
    drain(drs.at[pl.ds(1, NDEV - 1)], gr_s)
    drain(wgr, wg_s.at[0])
    drain(wg2.at[pl.ds(1, 63)], wg_s.at[1])


def table_kernel(ask_ref, drow_ref, out_ref):
    n = out_ref.shape[0]
    base = pl.program_id(0) * n
    hit = ask_ref[0:1, :] == lax.broadcasted_iota(I32, (n, NDEV * SLOTS), 0) + base
    mat = jnp.where(hit, F32(1), F32(0)).astype(BF)
    out_ref[...] = jnp.dot(mat, drow_ref[...], preferred_element_type=F32).astype(BF)


def local(user_vectors, item_table, tower_weight, item_owner, item_row):
    dma = pltpu.SemaphoreType.DMA
    vm = pl.BlockSpec(memory_space=pltpu.VMEM)
    n = NDEV * SLOTS
    scratch = [
        pltpu.VMEM((BD, D), BF),
        pltpu.VMEM((D, D), BF),
        pltpu.VMEM((1, BD), I32),
        pltpu.VMEM((1, BD), I32),
        pltpu.VMEM((ROWS, D), BF),
        pltpu.VMEM((8, 1, 128), I32),
        pltpu.VMEM((8, 1, 128), I32),
        pltpu.VMEM((16, 8, 1, 128), I32),
        pltpu.VMEM((n, 128), I32),
        pltpu.VMEM((NDEV, SLOTS, D), BF),
        pltpu.VMEM((NDEV, SLOTS, D), BF),
        pltpu.VMEM((NDEV, SLOTS, D), BF),
        pltpu.VMEM((NDEV, SLOTS, D), BF),
        pltpu.VMEM((8, BD, D), BF),
        pltpu.VMEM((BD, n), BF),
        pltpu.VMEM((n, BD), BF),
        pltpu.VMEM((BD, 8 * BD), BF),
        pltpu.VMEM((n, ROWS), BF),
        pltpu.VMEM((8, 64, D), BF),
        pltpu.VMEM((4, 64, D), BF),
        pltpu.VMEM((64, 4, D), BF),
        pltpu.VMEM((64, 4, D), BF),
        dma((5,)),
        dma((11,)),
        dma((11,)),
        dma((2,)),
        dma((2,)),
        dma,
        dma,
        dma,
        dma,
        dma((2,)),
        dma((2,)),
    ]
    drow, ask, wgrad = pl.pallas_call(
        step_kernel,
        out_shape=(
            jax.ShapeDtypeStruct((n, D), BF),
            jax.ShapeDtypeStruct((8, n), I32),
            jax.ShapeDtypeStruct((4, D), F32),
        ),
        in_specs=[pl.BlockSpec(memory_space=pl.ANY)] * 5,
        out_specs=(vm, vm, vm),
        scratch_shapes=scratch,
        compiler_params=pltpu.CompilerParams(
            collective_id=0, has_side_effects=True, vmem_limit_bytes=60 * 1024 * 1024
        ),
    )(user_vectors, item_table, tower_weight, item_owner.reshape(1, BD), item_row.reshape(1, BD))
    blk = 512
    tgrad = pl.pallas_call(
        table_kernel,
        grid=(ROWS // blk,),
        out_shape=jax.ShapeDtypeStruct((ROWS, D), BF),
        in_specs=[
            pl.BlockSpec((8, n), lambda i: (0, 0)),
            pl.BlockSpec((n, D), lambda i: (0, 0)),
        ],
        out_specs=pl.BlockSpec((blk, D), lambda i: (i, 0)),
    )(ask, drow)
    return tgrad, wgrad


def solution(mesh):
    return jax.shard_map(
        local,
        mesh=mesh,
        in_specs=(
            P(("batch", "item"), None),
            P(("batch", "item"), None),
            P(),
            P(("batch", "item"), None),
            P(("batch", "item")),
        ),
        out_specs=(P(("batch", "item"), None), P(("batch", "item"), None)),
        check_vma=False,
    )
```

time: 62.8 us -> 53.9 us (0.86)
  Pallas kernels: 61.4 us -> 52.5 us
    pallas_call x1, Pallas kernels: 55 us -> 46 us  [local(): pl.pallas_call(step_kernel, out_shape=(jax.ShapeDtypeStruct((n, D), BF),...]
where the time goes in v3:
time: 53.9 us; the launch traced here: 53.7 us
  Pallas kernels  52.5 us (97%)
  between operations  0.65 us (1%)
  local copies, waits for them, and re-layouts  0.6 us (1%)
    pallas_call x1, Pallas kernels, local(): pl.pallas_call(step_kernel, out_shape=(jax.ShapeDtypeStruct((n, D), BF),...  46 us
    pallas_call x1, Pallas kernels, local(): pl.pallas_call(table_kernel, grid=(ROWS // blk,), out_shape=jax.ShapeDtyp...  6.48 us

profile of v3, /device:TPU:0, one launch (start us, length us, event | category | flops | bytes accessed | tf_op | source)
XLA Modules:
  0.0 53.7 jit_solution(6794740490023349533)
XLA Ops:
  0.6 46.0 %shard_map.68 = (bf16[512,512]{1,0:T(8,128)(2,1)}, s32[8,512]{1,0:T(8,128)}, f32[4,512]{1,0:T(4,128)}) custom-call(bf16[256,512]{1,0:T(8,128)(2,1)} %user_ref.1, bf16[4096,512]{1,0:T(8,128)(2,1)} %table_ref.1, bf16[512,512]{1,0:T(8,128)(2,1)} %w_ref.1, s32[1,256]{1,0:T(1,128)} %bitcast.2, s32[1,256]{1,0:T(1,128)} %bitcast.3), custom_call_target="tpu_custom_call" | custom-call | tf_op jit(solution)/shard_map/pallas_call | solution.py:365
  46.6 0.0 copy-start
  46.7 6.5 %shard_map.69 = bf16[4096,512]{1,0:T(8,128)(2,1)} custom-call(s32[8,512]{1,0:T(8,128)} %get-tuple-element.5.ask_ref, bf16[512,512]{1,0:T(8,128)(2,1)} %get-tuple-element.6.drow_ref), custom_call_target="tpu_custom_call" | custom-call | tf_op jit(solution)/shard_map/pallas_call | solution.py:380
  53.1 0.0 copy-done
  53.1 0.6 %copy.8 = f32[4,512]{1,0:T(4,128)} copy(f32[4,512]{1,0:T(4,128)S(1)} %copy-done) | data formatting | bytes 16384
Async XLA Ops:
  46.6 6.5 %copy-start = (f32[4,512]{1,0:T(4,128)S(1)}, f32[4,512]{1,0:T(4,128)}, u32[]{:S(2)}) copy-start(f32[4,512]{1,0:T(4,128)} %get-tuple-element.11) | copy-start | bytes 24580

commit v4 on v3

--- a/solution.py
+++ b/solution.py
@@ -31,6 +31,18 @@
 
 def tn(a, b):
     return lax.dot_general(a, b, (((0,), (0,)), ((), ())), preferred_element_type=F32)
+
+
+def hops(i):
+    xi, ga, ze, et = (i % 8) // 2, i % 2, (i // 8) % 4, i // 32
+    return sum(min(k, 4 - k) for k in (xi, ze, et)) + 0.5 * ga
+
+
+def chunk(g):
+    return sorted([i for i in range(max(1, g * CH), (g + 1) * CH)], key=lambda i: -hops(i))
+
+
+ORDER = (2, 1, 3, 0)
 
 
 def step_kernel(
@@ -64,6 +76,9 @@
     wgr,
     wg2,
     wg3,
+    drn,
+    askv,
+    out_s,
     in_s,
     ag_s,
     ag_r,
@@ -147,11 +162,6 @@
     want = nt(high, spot) * 64.0 + nt(low, spot)
     req[...] = want.astype(I32).reshape(8, 1, 128)
 
-    pl.semaphore_wait(bar, 22)
-    for k in range(1, 8):
-        send(req.at[k], t1.at[k], rq_s.at[0], rq_r.at[0], at(k // 2, k % 2, 0, 0))
-    t1[0] = req[0]
-
     fetch[2].wait()
     uf = user_v[...].astype(F32)
     uu = (
@@ -160,6 +170,11 @@
         / jnp.sqrt(F32(D))
     ).astype(BF)
     ug[0] = uu
+    pl.semaphore_wait(bar, 22)
+    for k in range(1, 8):
+        send(req.at[k], t1.at[k], rq_s.at[0], rq_r.at[0], at(k // 2, k % 2, 0, 0))
+    t1[0] = req[0]
+
     h = BD // 2
     top, bot = pl.ds(0, h), pl.ds(h, h)
     right, left, other = at(1, 0, 0, 0), at(3, 0, 0, 0), at(0, 1, 0, 0)
@@ -174,7 +189,7 @@
     share(0, ug.at[0], ug.at[1], other)
 
     drain(t1.at[pl.ds(1, 7)], rq_r.at[0])
-    for k in range(1, 16):
+    for k in sorted(range(1, 16), key=lambda k: -hops(k * 8)):
         send(t1, asked.at[k], rq_s.at[1], rq_r.at[1], at(0, 0, k % 4, k // 4))
     asked[0] = t1[...]
 
@@ -193,6 +208,10 @@
     ones = jnp.ones((128, 128), BF)
     fetch[4].wait()
 
+    drain(ug.at[2, top], ag_r.at[1])
+    share(5, ug.at[2, top], ug.at[6, top], right)
+    drain(ug.at[4, bot], ag_r.at[3])
+    share(6, ug.at[4, bot], ug.at[6, bot], left)
     drain(asked.at[pl.ds(1, 15)], rq_r.at[1])
     parts = []
     for k in range(16):
@@ -209,7 +228,7 @@
         + jnp.dot(picked2, ones, preferred_element_type=F32)
     ).astype(I32)
 
-    for g in range(NCH):
+    for n, g in enumerate(ORDER):
         a = cols[g * CS : (g + 1) * CS, :]
         for j in range(ROWS // 128):
             hit = a == lax.broadcasted_iota(I32, (CS, 128), 1) + j * 128
@@ -220,32 +239,30 @@
             onehot[g * CS : (g + 1) * CS, :], table_v[...], preferred_element_type=F32
         )
         reply[g * CH : (g + 1) * CH] = found.astype(BF).reshape(CH, SLOTS, D)
-        for i in range(max(1, g * CH), (g + 1) * CH):
+        for i in chunk(g):
             xi, ga, ze, et = split(i)
             to = at(4 - xi, ga, 4 - ze, 4 - et)
             send(reply.at[i], emb.at[i], rp_s, rp_r, to)
-        if g == 0:
-            drain(ug.at[2, top], ag_r.at[1])
-            share(5, ug.at[2, top], ug.at[6, top], right)
-            drain(ug.at[4, bot], ag_r.at[3])
-            share(6, ug.at[4, bot], ug.at[6, bot], left)
-        if g == 1:
+        if n == 0:
             drain(ug.at[2, bot], ag_r.at[2])
             share(7, ug.at[2], ug.at[3], other)
             drain(ug.at[4, top], ag_r.at[4])
             share(8, ug.at[4], ug.at[5], other)
+        if n == 3:
+            drain(ug.at[6, top], ag_r.at[5])
+            share(9, ug.at[6, top], ug.at[7, top], other)
+            drain(ug.at[6, bot], ag_r.at[6])
+            share(10, ug.at[6, bot], ug.at[7, bot], other)
     emb[0] = reply[0]
     eye = lax.broadcasted_iota(I32, (128, 128), 0) == lax.broadcasted_iota(I32, (128, 128), 1)
     for g in range(NCH):
         a = cols[g * CS : (g + 1) * CS, :]
-        askrow_out[:, g * CS : (g + 1) * CS] = jnp.broadcast_to(
+        askv[:, g * CS : (g + 1) * CS] = jnp.broadcast_to(
             jnp.sum(jnp.where(eye, a, 0), axis=0, keepdims=True), (8, CS)
         )
 
-    drain(ug.at[6, top], ag_r.at[5])
-    share(9, ug.at[6, top], ug.at[7, top], other)
-    drain(ug.at[6, bot], ag_r.at[6])
-    share(10, ug.at[6, bot], ug.at[7, bot], other)
+    outs = [pltpu.make_async_copy(askv, askrow_out, out_s.at[0])]
+    outs[0].start()
     drain(ug.at[1], ag_r.at[0])
     drain(ug.at[3], ag_r.at[7])
     drain(ug.at[5], ag_r.at[8])
@@ -280,10 +297,10 @@
         send(wgs.at[k * 2 + 1 - c], wgr.at[k], wg_s.at[0], wg_r.at[0], other)
 
     drow = nt(dh, w_v[...]).astype(BF)
-    for g in range(NCH):
+    for g in ORDER:
         part = jnp.dot(forth[g * CS : (g + 1) * CS, :], drow, preferred_element_type=F32)
         drs[g * CH : (g + 1) * CH] = part.astype(BF).reshape(CH, SLOTS, D)
-        for i in range(max(1, g * CH), (g + 1) * CH):
+        for i in chunk(g):
             send(drs.at[i], dr.at[i], gr_s, gr_r, at(*split(i)))
     dr[0] = drs[0]
 
@@ -291,17 +308,21 @@
     for k in range(4):
         both = wgs[k * 2 + c].astype(F32) + wgr[k].astype(F32)
         wg2[k * 16 : (k + 1) * 16] = both.astype(BF).reshape(16, 4, D)
-    for j in range(1, 64):
+    for j in sorted(range(1, 64), key=lambda j: -hops(j // 16 * 2 + j // 4 % 4 * 8 + j % 4 * 32)):
         xi, ze, et = j // 16, (j // 4) % 4, j % 4
         src = wg2.at[xs[xi] * 8 + zs[ze] + ys[et]]
         send(src, wg3.at[j], wg_s.at[1], wg_r.at[1], at(xi, 0, ze, et))
     wg3[0] = wg2[x * 16 + z * 4 + y]
 
     drain(dr.at[pl.ds(1, NDEV - 1)], gr_r)
-    drow_out[...] = dr[...].reshape(NDEV * SLOTS, D)
+    drn[...] = dr[...].reshape(NDEV * SLOTS, D)
+    outs.append(pltpu.make_async_copy(drn, drow_out, out_s.at[1]))
+    outs[1].start()
     drain(wg3.at[pl.ds(1, 63)], wg_r.at[1])
     wg_out[...] = jnp.sum(wg3[...].astype(F32), axis=0)
 
+    for cp in outs:
+        cp.wait()
     drain(t1.at[pl.ds(1, 7)], rq_s.at[0])
     drain(asked.at[pl.ds(1, 15)], rq_s.at[1])
     drain(ug.at[0], ag_s.at[0])
@@ -315,17 +336,27 @@
     drain(wg2.at[pl.ds(1, 63)], wg_s.at[1])
 
 
-def table_kernel(ask_ref, drow_ref, out_ref):
-    n = out_ref.shape[0]
-    base = pl.program_id(0) * n
-    hit = ask_ref[0:1, :] == lax.broadcasted_iota(I32, (n, NDEV * SLOTS), 0) + base
-    mat = jnp.where(hit, F32(1), F32(0)).astype(BF)
-    out_ref[...] = jnp.dot(mat, drow_ref[...], preferred_element_type=F32).astype(BF)
+CUTS = (0, 256, 512, 768, 1024, 1280, 1536, 1792, 2048, 2304, 2560, 2816, 3072, 3328, 3584, 3840, 4096)
+
+
+def table_kernel(ask_ref, drow_ref, wg_ref, out_ref, wg_out, buf, sems):
+    copies = []
+    for k, (lo, hi) in enumerate(zip(CUTS[:-1], CUTS[1:])):
+        hit = ask_ref[0:1, :] == lax.broadcasted_iota(I32, (hi - lo, NDEV * SLOTS), 0) + lo
+        mat = jnp.where(hit, F32(1), F32(0)).astype(BF)
+        buf[lo:hi, :] = jnp.dot(mat, drow_ref[...], preferred_element_type=F32).astype(BF)
+        rows = pl.ds(lo, hi - lo)
+        copies.append(pltpu.make_async_copy(buf.at[rows], out_ref.at[rows], sems.at[k]))
+        copies[-1].start()
+    wg_out[...] = wg_ref[...]
+    for cp in copies:
+        cp.wait()
 
 
 def local(user_vectors, item_table, tower_weight, item_owner, item_row):
     dma = pltpu.SemaphoreType.DMA
     vm = pl.BlockSpec(memory_space=pltpu.VMEM)
+    hbm = pl.BlockSpec(memory_space=pl.ANY)
     n = NDEV * SLOTS
     scratch = [
         pltpu.VMEM((BD, D), BF),
@@ -350,6 +381,9 @@
         pltpu.VMEM((4, 64, D), BF),
         pltpu.VMEM((64, 4, D), BF),
         pltpu.VMEM((64, 4, D), BF),
+        pltpu.VMEM((n, D), BF),
+        pltpu.VMEM((8, n), I32),
+        dma((2,)),
         dma((5,)),
         dma((11,)),
         dma((11,)),
@@ -370,24 +404,22 @@
             jax.ShapeDtypeStruct((4, D), F32),
         ),
         in_specs=[pl.BlockSpec(memory_space=pl.ANY)] * 5,
-        out_specs=(vm, vm, vm),
+        out_specs=(hbm, hbm, vm),
         scratch_shapes=scratch,
         compiler_params=pltpu.CompilerParams(
             collective_id=0, has_side_effects=True, vmem_limit_bytes=60 * 1024 * 1024
         ),
     )(user_vectors, item_table, tower_weight, item_owner.reshape(1, BD), item_row.reshape(1, BD))
-    blk = 512
-    tgrad = pl.pallas_call(
+    return pl.pallas_call(
         table_kernel,
-        grid=(ROWS // blk,),
-        out_shape=jax.ShapeDtypeStruct((ROWS, D), BF),
-        in_specs=[
-            pl.BlockSpec((8, n), lambda i: (0, 0)),
-            pl.BlockSpec((n, D), lambda i: (0, 0)),
-        ],
-        out_specs=pl.BlockSpec((blk, D), lambda i: (i, 0)),
-    )(ask, drow)
-    return tgrad, wgrad
+        out_shape=(
+            jax.ShapeDtypeStruct((ROWS, D), BF),
+            jax.ShapeDtypeStruct((4, D), F32),
+        ),
+        in_specs=[vm, vm, vm],
+        out_specs=(hbm, vm),
+        scratch_shapes=[pltpu.VMEM((ROWS, D), BF), dma((len(CUTS) - 1,))],
+    )(ask, drow, wgrad)
 
 
 def solution(mesh):

time: 53.9 us -> 47.8 us (0.89)
  Pallas kernels: 52.5 us -> 47 us
  local copies, waits for them, and re-layouts: 0.6 us -> 0 us
    pallas_call x1, Pallas kernels: 46 us -> 42.2 us  [local(): pl.pallas_call(step_kernel, out_shape=(jax.ShapeDtypeStruct((n, D), BF),...]
    pallas_call x1, Pallas kernels: 6.48 us -> 4.83 us  [local(): pl.pallas_call(table_kernel, out_shape=(jax.ShapeDtypeStruct((ROWS, D), B...]
    unnamed x3 -> x0, local copies, waits for them, and re-layouts: 0.6 us -> none
where the time goes in v4:
time: 47.8 us; the launch traced here: 47.7 us
  Pallas kernels  47 us (98%)
  between operations  0.64 us (1%)
    pallas_call x1, Pallas kernels, local(): pl.pallas_call(step_kernel, out_shape=(jax.ShapeDtypeStruct((n, D), BF),...  42.2 us
    pallas_call x1, Pallas kernels, local(): pl.pallas_call(table_kernel, out_shape=(jax.ShapeDtypeStruct((ROWS, D), B...  4.83 us

profile of v4, /device:TPU:0, one launch (start us, length us, event | category | flops | bytes accessed | tf_op | source)
XLA Modules:
  0.0 47.7 jit_solution(7875669152598860678)
XLA Ops:
  0.6 42.2 %shard_map.68 = (bf16[512,512]{1,0:T(8,128)(2,1)}, s32[8,512]{1,0:T(8,128)}, f32[4,512]{1,0:T(4,128)}) custom-call(bf16[256,512]{1,0:T(8,128)(2,1)} %user_ref.1, bf16[4096,512]{1,0:T(8,128)(2,1)} %table_ref.1, bf16[512,512]{1,0:T(8,128)(2,1)} %w_ref.1, s32[1,256]{1,0:T(1,128)} %bitcast.2, s32[1,256]{1,0:T(1,128)} %bitcast.3), custom_call_target="tpu_custom_call" | custom-call | tf_op jit(solution)/shard_map/pallas_call | solution.py:399
  42.8 4.8 %shard_map.69 = (bf16[4096,512]{1,0:T(8,128)(2,1)}, f32[4,512]{1,0:T(4,128)}) custom-call(s32[8,512]{1,0:T(8,128)} %get-tuple-element.5.ask_ref, bf16[512,512]{1,0:T(8,128)(2,1)} %get-tuple-element.6.drow_ref, f32[4,512]{1,0:T(4,128)} %get-tuple-element.7.wg_ref), custom_call_target="tpu_custom_call" | custom-call | tf_op jit(solution)/shard_map/pallas_call | solution.py:413

commit v5 on v4

--- a/solution.py
+++ b/solution.py
@@ -66,7 +66,6 @@
     reply,
     emb,
     drs,
-    dr,
     ug,
     back,
     forth,
@@ -75,8 +74,6 @@
     wgs,
     wgr,
     wg2,
-    wg3,
-    drn,
     askv,
     out_s,
     in_s,
@@ -301,8 +298,9 @@
         part = jnp.dot(forth[g * CS : (g + 1) * CS, :], drow, preferred_element_type=F32)
         drs[g * CH : (g + 1) * CH] = part.astype(BF).reshape(CH, SLOTS, D)
         for i in chunk(g):
-            send(drs.at[i], dr.at[i], gr_s, gr_r, at(*split(i)))
-    dr[0] = drs[0]
+            send(drs.at[i], drow_out.at[i], gr_s, gr_r, at(*split(i)))
+    outs.append(pltpu.make_async_copy(drs.at[0], drow_out.at[0], out_s.at[1]))
+    outs[1].start()
 
     drain(wgr, wg_r.at[0])
     for k in range(4):
@@ -311,15 +309,14 @@
     for j in sorted(range(1, 64), key=lambda j: -hops(j // 16 * 2 + j // 4 % 4 * 8 + j % 4 * 32)):
         xi, ze, et = j // 16, (j // 4) % 4, j % 4
         src = wg2.at[xs[xi] * 8 + zs[ze] + ys[et]]
-        send(src, wg3.at[j], wg_s.at[1], wg_r.at[1], at(xi, 0, ze, et))
-    wg3[0] = wg2[x * 16 + z * 4 + y]
-
-    drain(dr.at[pl.ds(1, NDEV - 1)], gr_r)
-    drn[...] = dr[...].reshape(NDEV * SLOTS, D)
-    outs.append(pltpu.make_async_copy(drn, drow_out, out_s.at[1]))
-    outs[1].start()
-    drain(wg3.at[pl.ds(1, 63)], wg_r.at[1])
-    wg_out[...] = jnp.sum(wg3[...].astype(F32), axis=0)
+        send(src, wg_out.at[j], wg_s.at[1], wg_r.at[1], at(xi, 0, ze, et))
+    outs.append(
+        pltpu.make_async_copy(wg2.at[x * 16 + z * 4 + y], wg_out.at[0], out_s.at[2])
+    )
+    outs[2].start()
+
+    drain(drow_out.at[pl.ds(1, NDEV - 1)], gr_r)
+    drain(wg_out.at[pl.ds(1, 63)], wg_r.at[1])
 
     for cp in outs:
         cp.wait()
@@ -339,16 +336,21 @@
 CUTS = (0, 256, 512, 768, 1024, 1280, 1536, 1792, 2048, 2304, 2560, 2816, 3072, 3328, 3584, 3840, 4096)
 
 
-def table_kernel(ask_ref, drow_ref, wg_ref, out_ref, wg_out, buf, sems):
+def table_kernel(ask_ref, drow_ref, wg_ref, out_ref, wg_out, rows_v, wg_v, buf, sems):
+    bring = pltpu.make_async_copy(wg_ref, wg_v, sems.at[0])
+    bring.start()
+    rows_v[...] = drow_ref[...].reshape(NDEV * SLOTS, D)
     copies = []
     for k, (lo, hi) in enumerate(zip(CUTS[:-1], CUTS[1:])):
         hit = ask_ref[0:1, :] == lax.broadcasted_iota(I32, (hi - lo, NDEV * SLOTS), 0) + lo
         mat = jnp.where(hit, F32(1), F32(0)).astype(BF)
-        buf[lo:hi, :] = jnp.dot(mat, drow_ref[...], preferred_element_type=F32).astype(BF)
+        buf[lo:hi, :] = jnp.dot(mat, rows_v[...], preferred_element_type=F32).astype(BF)
         rows = pl.ds(lo, hi - lo)
-        copies.append(pltpu.make_async_copy(buf.at[rows], out_ref.at[rows], sems.at[k]))
+        copies.append(pltpu.make_async_copy(buf.at[rows], out_ref.at[rows], sems.at[k + 1]))
         copies[-1].start()
-    wg_out[...] = wg_ref[...]
+        if k == 8:
+            bring.wait()
+            wg_out[...] = jnp.sum(wg_v[...].astype(F32), axis=0)
     for cp in copies:
         cp.wait()
 
@@ -371,7 +373,6 @@
         pltpu.VMEM((NDEV, SLOTS, D), BF),
         pltpu.VMEM((NDEV, SLOTS, D), BF),
         pltpu.VMEM((NDEV, SLOTS, D), BF),
-        pltpu.VMEM((NDEV, SLOTS, D), BF),
         pltpu.VMEM((8, BD, D), BF),
         pltpu.VMEM((BD, n), BF),
         pltpu.VMEM((n, BD), BF),
@@ -380,10 +381,8 @@
         pltpu.VMEM((8, 64, D), BF),
         pltpu.VMEM((4, 64, D), BF),
         pltpu.VMEM((64, 4, D), BF),
-        pltpu.VMEM((64, 4, D), BF),
-        pltpu.VMEM((n, D), BF),
         pltpu.VMEM((8, n), I32),
-        dma((2,)),
+        dma((3,)),
         dma((5,)),
         dma((11,)),
         dma((11,)),
@@ -396,15 +395,15 @@
         dma((2,)),
         dma((2,)),
     ]
-    drow, ask, wgrad = pl.pallas_call(
+    drow, ask, shares = pl.pallas_call(
         step_kernel,
         out_shape=(
-            jax.ShapeDtypeStruct((n, D), BF),
+            jax.ShapeDtypeStruct((NDEV, SLOTS, D), BF),
             jax.ShapeDtypeStruct((8, n), I32),
-            jax.ShapeDtypeStruct((4, D), F32),
+            jax.ShapeDtypeStruct((64, 4, D), BF),
         ),
         in_specs=[pl.BlockSpec(memory_space=pl.ANY)] * 5,
-        out_specs=(hbm, hbm, vm),
+        out_specs=(hbm, hbm, hbm),
         scratch_shapes=scratch,
         compiler_params=pltpu.CompilerParams(
             collective_id=0, has_side_effects=True, vmem_limit_bytes=60 * 1024 * 1024
@@ -416,10 +415,15 @@
             jax.ShapeDtypeStruct((ROWS, D), BF),
             jax.ShapeDtypeStruct((4, D), F32),
         ),
-        in_specs=[vm, vm, vm],
+        in_specs=[vm, vm, hbm],
         out_specs=(hbm, vm),
-        scratch_shapes=[pltpu.VMEM((ROWS, D), BF), dma((len(CUTS) - 1,))],
-    )(ask, drow, wgrad)
+        scratch_shapes=[
+            pltpu.VMEM((n, D), BF),
+            pltpu.VMEM((64, 4, D), BF),
+            pltpu.VMEM((ROWS, D), BF),
+            dma((len(CUTS),)),
+        ],
+    )(ask, drow, shares)
 
 
 def solution(mesh):

time: 47.8 us -> 47.6 us (level)
    pallas_call x1, Pallas kernels: 42.2 us -> 41.6 us  [local(): pl.pallas_call(step_kernel, out_shape=(jax.ShapeDtypeStruct((NDEV, SLOTS,...]
where the time goes in v5:
time: 47.6 us; the launch traced here: 47.4 us
  Pallas kernels  46.7 us (98%)
  between operations  0.64 us (1%)
    pallas_call x1, Pallas kernels, local(): pl.pallas_call(step_kernel, out_shape=(jax.ShapeDtypeStruct((NDEV, SLOTS,...  41.6 us
    pallas_call x1, Pallas kernels, local(): pl.pallas_call(table_kernel, out_shape=(jax.ShapeDtypeStruct((ROWS, D), B...  5.12 us

profile of v5, /device:TPU:0, one launch (start us, length us, event | category | flops | bytes accessed | tf_op | source)
XLA Modules:
  0.0 47.4 jit_solution(9383687241104181566)
XLA Ops:
  0.6 41.6 %shard_map.68 = (bf16[128,4,512]{2,1,0:T(4,128)(2,1)}, s32[8,512]{1,0:T(8,128)}, bf16[64,4,512]{2,1,0:T(4,128)(2,1)}) custom-call(bf16[256,512]{1,0:T(8,128)(2,1)} %user_ref.1, bf16[4096,512]{1,0:T(8,128)(2,1)} %table_ref.1, bf16[512,512]{1,0:T(8,128)(2,1)} %w_ref.1, s32[1,256]{1,0:T(1,128)} %bitcast.2, s32[1,256]{1,0:T(1,128)} %bitcast.3), custom_call_target="tpu_custom_call" | custom-call | tf_op jit(solution)/shard_map/pallas_call | solution.py:398
  42.2 5.1 %shard_map.69 = (bf16[4096,512]{1,0:T(8,128)(2,1)}, f32[4,512]{1,0:T(4,128)}) custom-call(s32[8,512]{1,0:T(8,128)} %get-tuple-element.5.ask_ref, bf16[128,4,512]{2,1,0:T(4,128)(2,1)} %get-tuple-element.6.drow_ref, bf16[64,4,512]{2,1,0:T(4,128)(2,1)} %get-tuple-element.7.wg_ref), custom_call_target="tpu_custom_call" | custom-call | tf_op jit(solution)/shard_map/pallas_call | solution.py:412

commit v6 on v5

--- a/solution.py
+++ b/solution.py
@@ -122,13 +122,16 @@
             ]
         )
     ]
-    for cp in fetch:
+    for cp in fetch[:2]:
         cp.start()
     bar = pltpu.get_barrier_semaphore()
     for k in range(1, 8):
         pl.semaphore_signal(bar, inc=1, device_id=at(k // 2, k % 2, 0, 0), device_id_type=MESH)
     for k in range(1, 16):
         pl.semaphore_signal(bar, inc=1, device_id=at(0, 0, k % 4, k // 4), device_id_type=MESH)
+
+    for cp in fetch[2:]:
+        cp.start()
 
     fetch[0].wait()
     fetch[1].wait()
@@ -159,6 +162,11 @@
     want = nt(high, spot) * 64.0 + nt(low, spot)
     req[...] = want.astype(I32).reshape(8, 1, 128)
 
+    pl.semaphore_wait(bar, 22)
+    for k in range(1, 8):
+        send(req.at[k], t1.at[k], rq_s.at[0], rq_r.at[0], at(k // 2, k % 2, 0, 0))
+    t1[0] = req[0]
+
     fetch[2].wait()
     uf = user_v[...].astype(F32)
     uu = (
@@ -167,11 +175,6 @@
         / jnp.sqrt(F32(D))
     ).astype(BF)
     ug[0] = uu
-    pl.semaphore_wait(bar, 22)
-    for k in range(1, 8):
-        send(req.at[k], t1.at[k], rq_s.at[0], rq_r.at[0], at(k // 2, k % 2, 0, 0))
-    t1[0] = req[0]
-
     h = BD // 2
     top, bot = pl.ds(0, h), pl.ds(h, h)
     right, left, other = at(1, 0, 0, 0), at(3, 0, 0, 0), at(0, 1, 0, 0)
@@ -333,7 +336,7 @@
     drain(wg2.at[pl.ds(1, 63)], wg_s.at[1])
 
 
-CUTS = (0, 256, 512, 768, 1024, 1280, 1536, 1792, 2048, 2304, 2560, 2816, 3072, 3328, 3584, 3840, 4096)
+CUTS = (0, 128, 256, 512, 768, 1024, 1280, 1536, 1792, 2048, 2304, 2560, 2816, 3072, 3328, 3584, 3840, 4096)
 
 
 def table_kernel(ask_ref, drow_ref, wg_ref, out_ref, wg_out, rows_v, wg_v, buf, sems):

time: 47.6 us -> 47.6 us (level)
  no operation moved by 1% of the time
where the time goes in v6:
time: 47.6 us; the launch traced here: 47.4 us
  Pallas kernels  46.8 us (98%)
  between operations  0.64 us (1%)
    pallas_call x1, Pallas kernels, local(): pl.pallas_call(step_kernel, out_shape=(jax.ShapeDtypeStruct((NDEV, SLOTS,...  41.6 us
    pallas_call x1, Pallas kernels, local(): pl.pallas_call(table_kernel, out_shape=(jax.ShapeDtypeStruct((ROWS, D), B...  5.15 us

profile of v6, /device:TPU:0, one launch (start us, length us, event | category | flops | bytes accessed | tf_op | source)
XLA Modules:
  0.0 47.4 jit_solution(13878730673155708457)
XLA Ops:
  0.6 41.6 %shard_map.68 = (bf16[128,4,512]{2,1,0:T(4,128)(2,1)}, s32[8,512]{1,0:T(8,128)}, bf16[64,4,512]{2,1,0:T(4,128)(2,1)}) custom-call(bf16[256,512]{1,0:T(8,128)(2,1)} %user_ref.1, bf16[4096,512]{1,0:T(8,128)(2,1)} %table_ref.1, bf16[512,512]{1,0:T(8,128)(2,1)} %w_ref.1, s32[1,256]{1,0:T(1,128)} %bitcast.2, s32[1,256]{1,0:T(1,128)} %bitcast.3), custom_call_target="tpu_custom_call" | custom-call | tf_op jit(solution)/shard_map/pallas_call | solution.py:401
  42.3 5.2 %shard_map.69 = (bf16[4096,512]{1,0:T(8,128)(2,1)}, f32[4,512]{1,0:T(4,128)}) custom-call(s32[8,512]{1,0:T(8,128)} %get-tuple-element.5.ask_ref, bf16[128,4,512]{2,1,0:T(4,128)(2,1)} %get-tuple-element.6.drow_ref, bf16[64,4,512]{2,1,0:T(4,128)(2,1)} %get-tuple-element.7.wg_ref), custom_call_target="tpu_custom_call" | custom-call | tf_op jit(solution)/shard_map/pallas_call | solution.py:415
